TPU v7x, 256 devices: a whole 4x4x8 slice. The times are simulated.
256 devices in a mesh: pair: 32 (over z_hi, x, core), row: 8 (over y, z_lo).
Axes of the slice: x: 4, y: 4, z: 8 (z_hi: 4, z_lo: 2; z = z_hi * 2 + z_lo), core: 2. Of those that a mesh axis runs over, the one named last changes fastest.
Arguments:
- gram_field: float32 [128, 8, 16, 16, 256], P('pair', None, 'row'), may hold values from -3.6 to 3.6, as said below
- left_variance: float32 [128, 16, 16], P('pair'), may hold values from 0.25 to 4
- right_variance: float32 [8, 16, 16], replicated, may hold values from 0.25 to 4
- cotangent: float32 [128, 8, 8, 8, 64], P('pair', 'row'), may hold values from -24 to 24
Outputs:
- gram_gradient: float32 [128, 8, 16, 16, 256], P('pair', None, 'row')
- left_gradient: float32 [128, 16, 16], P('pair')
- right_gradient: float32 [8, 16, 16], replicated
Inputs may be any that keep to these rules, and one draw needn't show every extreme that they name: `gram_field`: each entry lies within 0.9 times the square root of the product of left_variance and right_variance at its two pixels.
All inputs are finite; a program needn't handle non-finite values.
Results may differ from a plain program's by a relative error of at most 0.00008.
Values sent between devices are 32-bit elements; how exact they have to be, the bound alone decides.
No kernel may reach another device: no remote copies, remote signals or barrier semaphores. Data moves between devices by JAX's collectives and lax.ppermute only.
A program may use at most 64 MiB of HBM per device.

v0:
```python
import jax
import jax.numpy as jnp
from jax import lax
from jax.sharding import PartitionSpec as P


def padded_2(block, sides, width):
    for axis, dim in sides:
        count = lax.axis_size(axis)
        forward = [(i, i + 1) for i in range(count - 1)]
        backward = [(target, source) for source, target in forward]
        low = lax.ppermute(
            lax.slice_in_dim(block, block.shape[dim] - width, None, axis=dim), axis, forward
        )
        high = lax.ppermute(lax.slice_in_dim(block, 0, width, axis=dim), axis, backward)
        block = jnp.concatenate([low, block, high], axis=dim)
    return block


def shifted(source, dimension, offset):
    dimension = dimension % source.ndim
    extent = source.shape[dimension]
    margin = abs(offset)
    widths = [(0, 0)] * source.ndim
    widths[dimension] = (margin, margin)
    padded = jnp.pad(source, widths)
    return lax.slice_in_dim(padded, margin + offset, margin + offset + extent, axis=dimension)


def column_masks(length):
    column_index = jnp.arange(length * length) % length
    return (
        (column_index + 1 < length).astype(jnp.float32),
        (column_index >= 1).astype(jnp.float32),
    )


def mix_columns(source, length):
    mask_up, mask_down = column_masks(length)
    return (
        source
        + shifted(shifted(source, -2, 1), -1, 1) * mask_up
        + shifted(shifted(source, -2, -1), -1, -1) * mask_down
    )


def conv_field(padded, length):
    inner = (
        padded[..., 1:-1, :, :]
        + shifted(padded[..., 2:, :, :], -1, length)
        + shifted(padded[..., :-2, :, :], -1, -length)
    )
    return mix_columns(inner, length) / 9.0


def pad_rows(source):
    widths = [(0, 0)] * source.ndim
    widths[source.ndim - 3] = (1, 1)
    return jnp.pad(source, widths)


def conv_map(source):
    row_sum = source + shifted(source, -2, 1) + shifted(source, -2, -1)
    return (row_sum + shifted(row_sum, -1, 1) + shifted(row_sum, -1, -1)) / 9.0


def pool_field(source):
    shape = source.shape
    leading = shape[:-3]
    count = shape[-3]
    length = shape[-2]
    half_side = length // 2
    merged = source.reshape(shape[:-1] + (half_side, 2 * length))
    merged = merged[..., :length] + merged[..., length:]
    merged = merged.reshape(shape[:-1] + (half_side * length,))
    merged = merged[..., 0::2] + merged[..., 1::2]
    merged = merged.reshape(leading + (count // 2, 2, half_side, 2, half_side * half_side))
    return jnp.sum(merged, axis=(-4, -2)) / 16.0


def spread_field(source):
    half_side = source.shape[-2]
    merged = jnp.repeat(source, 2, axis=-3)
    merged = jnp.repeat(merged, 2, axis=-2)
    inner = merged.shape[:-1]
    merged = merged.reshape(inner + (half_side, 1, half_side, 1))
    merged = jnp.broadcast_to(merged, inner + (half_side, 2, half_side, 2))
    return merged.reshape(inner + (4 * half_side * half_side,)) / 16.0


def pool_map(source):
    extent = source.shape[-1] // 2
    merged = source.reshape(source.shape[:-2] + (extent, 2, extent, 2))
    return jnp.mean(merged, axis=(-3, -1))


def spread_map(source):
    return jnp.repeat(jnp.repeat(source, 2, axis=-2), 2, axis=-1) / 4.0


def arc_kernel(source, left, right):
    magnitude = jnp.sqrt(left * right)
    cosine = source / magnitude
    angle_part = jnp.pi - jnp.arccos(cosine)
    sine_part = jnp.sqrt(1.0 - cosine * cosine)
    kernel = magnitude * (sine_part + angle_part * cosine) / (2.0 * jnp.pi)
    slopes = angle_part / (2.0 * jnp.pi)
    weights = magnitude * sine_part / (4.0 * jnp.pi)
    return (kernel, slopes, weights)


def row_window(source, first, count):
    padded = jnp.pad(source, ((0, 0), (2, 2), (0, 0)), constant_values=1.0)
    return lax.dynamic_slice_in_dim(padded, first + 2, count, axis=1)


def on_device(gram_field, left_variance, right_variance, cotangent):
    left_count = gram_field.shape[0]
    shard_rows = gram_field.shape[2]
    length = gram_field.shape[3]
    half_side = length // 2
    count = right_variance.shape[0]
    part_count = cotangent.shape[1]
    rank = lax.axis_index("row")
    zero = rank * 0
    start = rank * shard_rows
    first_left = conv_map(left_variance)
    first_right = conv_map(right_variance)
    right_flat = first_right.reshape(1, count, 1, 1, length * length)
    second_left = conv_map(pool_map(first_left / 2.0))
    second_right = conv_map(pool_map(first_right / 2.0)).reshape(count, half_side * half_side)
    padded = padded_2(gram_field, (("row", 2),), 1)
    source_one = conv_field(padded, length)
    left_rows = row_window(first_left, start, shard_rows)
    kernel_one, slope_one, weight_one = arc_kernel(
        source_one, left_rows[:, None, :, :, None], right_flat
    )
    pooled = pool_field(kernel_one)
    gathered = lax.all_to_all(pooled, "row", split_axis=1, concat_axis=2, tiled=True)
    source_two = conv_field(pad_rows(gathered), half_side)
    first_image = rank * part_count
    second_part = lax.dynamic_slice_in_dim(second_right, first_image, part_count, axis=0)
    unused, slope_two, weight_two = arc_kernel(
        source_two, second_left[:, None, :, :, None], second_part[None, :, None, None, :]
    )
    weighted_two = cotangent * weight_two
    left_two = jnp.sum(weighted_two, axis=(1, 4)) / second_left
    right_part = jnp.sum(weighted_two, axis=(0, 2, 3)) / second_part
    right_two = lax.dynamic_update_slice(
        jnp.zeros((count, half_side * half_side), jnp.float32), right_part, (first_image, zero)
    )
    back_local = conv_field(pad_rows(cotangent * slope_two), half_side)
    back_pooled = lax.all_to_all(back_local, "row", split_axis=2, concat_axis=1, tiled=True)
    back_one = spread_field(back_pooled)
    grad_padded = padded_2(back_one * slope_one, (("row", 2),), 1)
    gram_gradient = conv_field(grad_padded, length)
    weighted_one = back_one * weight_one
    left_local = jnp.sum(weighted_one, axis=(1, 4)) / left_rows
    left_placed = lax.dynamic_update_slice(
        jnp.zeros((left_count, length, length), jnp.float32), left_local, (zero, start, zero)
    )
    left_one = spread_map(conv_map(left_two)) / 2.0 + left_placed
    right_local = jnp.sum(weighted_one, axis=(0, 2, 3)) / first_right.reshape(
        count, length * length
    )
    right_one = spread_map(
        conv_map(right_two.reshape(count, half_side, half_side))
    ) / 2.0 + right_local.reshape(count, length, length)
    left_total = lax.psum(left_one, "row")
    right_total = lax.psum(right_one, ("pair", "row"))
    return (gram_gradient, conv_map(left_total), conv_map(right_total))


def solution(mesh):
    in_specs = (
        P("pair", None, "row", None, None),
        P("pair", None, None),
        P(),
        P("pair", "row", None, None, None),
    )
    out_specs = (P("pair", None, "row", None, None), P("pair", None, None), P())
    return jax.shard_map(
        on_device, mesh=mesh, in_specs=in_specs, out_specs=out_specs, check_vma=False
    )
```

profile of v0, /device:TPU:2, one launch (start us, length us, event | category | flops | bytes accessed | tf_op | source)
XLA Modules:
  0.0 249.3 jit_solution(6002898076283991373)
XLA Ops:
  0.7 2.2 fusion.66
  2.8 3.8 %collective-permute-start.1 = (f32[4,8,1,16,256]{4,3,2,1,0:T(8,128)}, f32[4,8,1,16,256]{4,3,2,1,0:T(8,128)S(1)}, u32[]{:S(2)}, u32[]{:S(2)}) collective-permute-start(f32[4,8,1,16,256]{4,3,2,1,0:T(8,128)} %get-tuple-element.41), channel_id=1, source_target_pairs={{0,1},{1,2},{2,3},{3,4},{4,5},{5,6},{6,7},{8,9},{9,10},{10,11},{11... | collective-permute-start | bytes 1572872 | tf_op jit(solution)/shard_map/ppermute | solution.py:12
  6.7 1.3 collective-permute-start
  9.0 9.2 %collective-permute-done.1 = f32[4,8,1,16,256]{4,3,2,1,0:T(8,128)S(1)} collective-permute-done((f32[4,8,1,16,256]{4,3,2,1,0:T(8,128)}, f32[4,8,1,16,256]{4,3,2,1,0:T(8,128)S(1)}, u32[]{:S(2)}, u32[]{:S(2)}) %collective-permute-start.1) | collective-permute-done | bytes 524320 | tf_op jit(solution)/shard_map/ppermute | solution.py:12
  18.1 12.7 %collective-permute-done = f32[4,8,1,16,256]{4,3,2,1,0:T(8,128)S(1)} collective-permute-done((f32[4,8,1,16,256]{4,3,2,1,0:T(8,128)S(1)}, f32[4,8,1,16,256]{4,3,2,1,0:T(8,128)S(1)}, u32[]{:S(2)}, u32[]{:S(2)}) %collective-permute-start) | collective-permute-done | bytes 524320 | tf_op jit(solution)/shard_map/ppermute | solution.py:15
  30.9 0.8 copy-done.3
  32.5 0.8 copy-done.2
  33.5 4.2 %multiply_multiply_fusion.1 = (f32[4,8,2,16,256]{4,3,2,1,0:T(8,128)}, f32[4,8,2,16,256]{4,3,2,1,0:T(8,128)S(1)}) fusion(f32[8,256]{1,0:T(8,128)S(1)} %copy.153, f32[4,2,16]{2,1,0:T(2,128)S(1)} %pad_dynamic-slice_fusion, f32[256]{0:T(256)S(1)} %get-tuple-element.56, f32[4,8,2,16,256]{4,3,2,1,0:T(8,128)S(1)} %get-tuple-element.39, ...), kind=kLoop, calls=%fused_computation.43 | loop fusion | flops 8650752 | bytes 6302208 | tf_op jit(solution)/shard_map/div | solution.py:106
  37.7 3.7 %reshape.132 = f32[4,8,2,16,8,32]{5,4,3,2,1,0:T(8,128)} reshape(f32[4,8,2,16,256]{4,3,2,1,0:T(8,128)} %get-tuple-element.31) | data formatting | bytes 2097152 | tf_op jit(solution)/shard_map/reshape | solution.py:73
  41.4 6.6 %slice_add_fusion = f32[4,8,2,16,8,16]{5,4,3,2,1,0:T(8,128)} fusion(f32[4,8,2,16,8,32]{5,4,3,2,1,0:T(8,128)} %reshape.132), kind=kLoop, calls=%fused_computation | loop fusion | flops 131072 | bytes 1572864 | tf_op jit(solution)/shard_map/add | solution.py:74
  48.0 3.2 %reshape.133 = f32[4,8,2,16,128]{4,3,2,1,0:T(8,128)S(1)} reshape(f32[4,8,2,16,8,16]{5,4,3,2,1,0:T(8,128)} %slice_add_fusion) | data formatting | bytes 1048576 | tf_op jit(solution)/shard_map/reshape | solution.py:75
  51.3 11.2 %slice.242 = f32[4,8,2,16,64]{4,3,2,1,0:T(8,128)S(1)} slice(f32[4,8,2,16,128]{4,3,2,1,0:T(8,128)S(1)} %reshape.133), slice={[0:4:1], [0:8:1], [0:2:1], [0:16:1], [0:128:2]} | slice | bytes 524288 | tf_op jit(solution)/shard_map/slice | solution.py:76
  62.4 11.3 %slice.243 = f32[4,8,2,16,64]{4,3,2,1,0:T(8,128)S(1)} slice(f32[4,8,2,16,128]{4,3,2,1,0:T(8,128)S(1)} %reshape.133), slice={[0:4:1], [0:8:1], [0:2:1], [0:16:1], [1:128:2]} | slice | bytes 524288 | tf_op jit(solution)/shard_map/slice | solution.py:76
  75.0 5.5 %all-to-all-start = ((f32[8,1,2048]{2,1,0:T(1,128)}), f32[8,1,2048]{2,1,0:T(1,128)S(1)}, u32[]{:S(2)}, u32[]{:S(2)}) async-start(f32[8,1,2048]{2,1,0:T(1,128)} %reshape.138), calls=%async_computation | async-start | bytes 131072 | tf_op jit(solution)/shard_map/all_to_all | solution.py:139
  80.8 6.1 %all-to-all-done = f32[8,1,2048]{2,1,0:T(1,128)S(1)} async-done(((f32[8,1,2048]{2,1,0:T(1,128)}), f32[8,1,2048]{2,1,0:T(1,128)S(1)}, u32[]{:S(2)}, u32[]{:S(2)}) %all-to-all-start) | async-done | bytes 65568 | tf_op jit(solution)/shard_map/all_to_all | solution.py:139
  87.4 0.8 reduce.4
  90.2 3.4 %all-to-all-start.1 = ((f32[8,1,2048]{2,1,0:T(1,128)}), f32[8,1,2048]{2,1,0:T(1,128)S(1)}, u32[]{:S(2)}, u32[]{:S(2)}) async-start(f32[8,1,2048]{2,1,0:T(1,128)} %reshape.140), calls=%async_computation.1 | async-start | bytes 131072 | tf_op jit(solution)/shard_map/all_to_all | solution.py:153
  96.0 3.9 %all-to-all-done.1 = f32[8,1,2048]{2,1,0:T(1,128)S(1)} async-done(((f32[8,1,2048]{2,1,0:T(1,128)}), f32[8,1,2048]{2,1,0:T(1,128)S(1)}, u32[]{:S(2)}, u32[]{:S(2)}) %all-to-all-start.1) | async-done | bytes 65568 | tf_op jit(solution)/shard_map/all_to_all | solution.py:153
  99.8 0.8 reduce.5
  102.1 2.2 copy.171
  104.3 3.5 %broadcast_in_dim.45 = f32[4,8,16,8,2,8,2]{2,1,6,5,4,3,0:T(8,128)} broadcast(f32[4,8,16,8,8]{2,1,4,3,0:T(8,128)} %copy.171), dimensions={0,1,2,3,5} | broadcast | bytes 655360 | tf_op jit(solution)/shard_map/broadcast_in_dim | solution.py:87
  107.8 3.6 %copy.172 = f32[4,8,16,256]{3,2,1,0:T(8,128)} copy(f32[4,8,16,256]{2,1,3,0:T(8,128)} %bitcast.51) | data formatting | bytes 1048576 | tf_op jit(solution)/shard_map/mul | solution.py:157
  112.1 2.2 copy.163
  114.2 3.5 %broadcast_in_dim.19 = f32[4,8,16,8,2,8,2]{2,1,6,5,4,3,0:T(8,128)} broadcast(f32[4,8,16,8,8]{2,1,4,3,0:T(8,128)} %copy.163), dimensions={0,1,2,3,5} | broadcast | bytes 655360 | tf_op jit(solution)/shard_map/broadcast_in_dim | solution.py:87
  117.8 2.8 %copy.164 = f32[4,8,16,256]{3,2,1,0:T(8,128)S(1)} copy(f32[4,8,16,256]{2,1,3,0:T(8,128)} %bitcast.52) | data formatting | bytes 1048576 | tf_op jit(solution)/shard_map/mul | solution.py:155
  120.6 2.7 %fusion.26 = (f32[8,256]{1,0:T(8,128)S(1)}, f32[4,2,16]{2,1,0:T(2,128)S(1)}, f32[4,8,2,16,256]{4,3,2,1,0:T(8,128)S(1)}) fusion(f32[4,8,2,16,256]{4,3,2,1,0:T(8,128)S(1)} %get-tuple-element.32, f32[4,8,16,256]{3,2,1,0:T(8,128)S(1)} %copy-done.5, f32[8,256]{1,0:T(8,128)S(1)} %copy.153, f32[4,2,16]{2,1,0:T(2,128)S(1)} %pad_dynamic-slice_fusion, ...), kind=kLoop, calls=%fused_computation.50 | loop fusion | flops 3143552 | bytes 3163136 | tf_op jit(solution)/shard_map/reduce_sum | solution.py:163
  123.4 0.9 fusion.65
  124.2 2.7 %collective-permute-start.3 = (f32[4,8,1,16,256]{4,3,2,1,0:T(8,128)}, f32[4,8,1,16,256]{4,3,2,1,0:T(8,128)S(1)}, u32[]{:S(2)}, u32[]{:S(2)}) collective-permute-start(f32[4,8,1,16,256]{4,3,2,1,0:T(8,128)} %get-tuple-element.37), channel_id=1, source_target_pairs={{0,1},{1,2},{2,3},{3,4},{4,5},{5,6},{6,7},{8,9},{9,10},{10,11},{11... | collective-permute-start | bytes 1572872 | tf_op jit(solution)/shard_map/ppermute | solution.py:12
  126.9 1.3 collective-permute-start.2
  128.4 81.4 %psum.15 = f32[8,16,16]{0,2,1:T(8,128)S(1)} all-reduce(f32[8,16,16]{0,2,1:T(8,128)S(1)} %divide_add_fusion), channel_id=1, replica_groups=mesh['pair'=32,'row'=8] {'pair','row'}, use_global_device_ids=true, to_apply=%region_9.10 | all-reduce | flops 2048 | bytes 16384 | tf_op jit(solution)/shard_map/psum | solution.py:170
  210.6 34.6 %psum.14 = f32[4,16,16]{2,1,0:T(8,128)S(1)} all-reduce(f32[4,16,16]{2,1,0:T(8,128)S(1)} %add_dynamic-update-slice_fusion), channel_id=1, replica_groups=mesh['pair'=32,'row'=8] {'row'}, use_global_device_ids=true, to_apply=%region_6.7 | all-reduce | flops 1024 | bytes 8192 | tf_op jit(solution)/shard_map/psum | solution.py:169
  247.2 2.1 fusion.9
  (111 shorter events, 13.2 us)
Async XLA Ops:
  0.6 31.0 %copy-start = (f32[4,8,2,16,256]{4,3,2,1,0:T(8,128)S(1)}, f32[4,8,2,16,256]{4,3,2,1,0:T(8,128)}, u32[]{:S(2)}) copy-start(f32[4,8,2,16,256]{4,3,2,1,0:T(8,128)} %param.4) | copy-start | bytes 3145732
  0.6 7.4 %copy-start.12 = (f32[8,16,16]{2,1,0:T(8,128)S(1)}, f32[8,16,16]{2,1,0:T(8,128)}, u32[]{:S(2)}) copy-start(f32[8,16,16]{2,1,0:T(8,128)} %param.6) | copy-start | bytes 24580
  0.7 7.6 %copy-start.13 = (f32[4,16,16]{2,1,0:T(8,128)S(1)}, f32[4,16,16]{2,1,0:T(8,128)}, u32[]{:S(2)}) copy-start(f32[4,16,16]{2,1,0:T(8,128)} %param.5) | copy-start | bytes 12292
  2.8 15.3 %collective-permute-start.1 = (f32[4,8,1,16,256]{4,3,2,1,0:T(8,128)}, f32[4,8,1,16,256]{4,3,2,1,0:T(8,128)S(1)}, u32[]{:S(2)}, u32[]{:S(2)}) collective-permute-start(f32[4,8,1,16,256]{4,3,2,1,0:T(8,128)} %get-tuple-element.41), channel_id=1, source_target_pairs={{0,1},{1,2},{2,3},{3,4},{4,5},{5,6},{6,7},{8,9},{9,10},{10,11},{11... | collective-permute-start | bytes 1572872 | tf_op jit(solution)/shard_map/ppermute | solution.py:12
  6.7 24.2 %collective-permute-start = (f32[4,8,1,16,256]{4,3,2,1,0:T(8,128)S(1)}, f32[4,8,1,16,256]{4,3,2,1,0:T(8,128)S(1)}, u32[]{:S(2)}, u32[]{:S(2)}) collective-permute-start(f32[4,8,1,16,256]{4,3,2,1,0:T(8,128)S(1)} %get-tuple-element.40), channel_id=1, source_target_pairs={{1,0},{2,1},{3,2},{4,3},{5,4},{6,5},{7,6},{9,8},{10,9},{11,10},{12... | collective-permute-start | bytes 1572872 | tf_op jit(solution)/shard_map/ppermute | solution.py:15
  8.4 24.1 %copy-start.9 = (f32[4,16,16]{2,1,0:T(8,128)}, f32[4,16,16]{2,1,0:T(8,128)S(1)}, u32[]{:S(2)}) copy-start(f32[4,16,16]{2,1,0:T(8,128)S(1)} %get-tuple-element.53) | copy-start | bytes 12292
  8.9 23.6 %copy-start.14 = (f32[256]{0:T(256)}, f32[256]{0:T(256)S(1)}, u32[]{:S(2)}) copy-start(f32[256]{0:T(256)S(1)} %get-tuple-element.57) | copy-start | bytes 3076
  18.1 12.7 %copy-start.1 = (f32[4,8,1,16,256]{4,3,2,1,0:T(8,128)}, f32[4,8,1,16,256]{4,3,2,1,0:T(8,128)S(1)}, u32[]{:S(2)}) copy-start(f32[4,8,1,16,256]{4,3,2,1,0:T(8,128)S(1)} %collective-permute-done.1) | copy-start | bytes 1572868
  30.9 0.8 copy-start.3
  32.3 1.0 copy-start.2
  32.3 1.2 copy-start.4
  73.8 14.7 %copy-start.7 = (f32[4,1,8,8,64]{4,3,2,1,0:T(8,128)S(1)}, f32[4,1,8,8,64]{4,3,2,1,0:T(8,128)}, u32[]{:S(2)}) copy-start(f32[4,1,8,8,64]{4,3,2,1,0:T(8,128)} %param.7) | copy-start | bytes 196612
  75.0 11.9 %all-to-all-start = ((f32[8,1,2048]{2,1,0:T(1,128)}), f32[8,1,2048]{2,1,0:T(1,128)S(1)}, u32[]{:S(2)}, u32[]{:S(2)}) async-start(f32[8,1,2048]{2,1,0:T(1,128)} %reshape.138), calls=%async_computation | async-start | bytes 131072 | tf_op jit(solution)/shard_map/all_to_all | solution.py:139
  90.2 9.6 %all-to-all-start.1 = ((f32[8,1,2048]{2,1,0:T(1,128)}), f32[8,1,2048]{2,1,0:T(1,128)S(1)}, u32[]{:S(2)}, u32[]{:S(2)}) async-start(f32[8,1,2048]{2,1,0:T(1,128)} %reshape.140), calls=%async_computation.1 | async-start | bytes 131072 | tf_op jit(solution)/shard_map/all_to_all | solution.py:153
  107.8 3.6 %copy-start.6 = (f32[4,8,8,64]{3,2,0,1:T(8,128)S(1)}, f32[4,8,8,64]{3,2,0,1:T(8,128)}, u32[]{:S(2)}) copy-start(f32[4,8,8,64]{3,2,0,1:T(8,128)} %get-tuple-element.43) | copy-start | bytes 196612
  117.8 2.9 %copy-start.5 = (f32[4,8,16,256]{3,2,1,0:T(8,128)S(1)}, f32[4,8,16,256]{3,2,1,0:T(8,128)}, u32[]{:S(2)}) copy-start(f32[4,8,16,256]{3,2,1,0:T(8,128)} %copy.172) | copy-start | bytes 1572868
  120.6 7.7 %copy-start.8 = (f32[8,16,16]{0,2,1:T(8,128)S(1)}, f32[8,16,16]{0,2,1:T(8,128)}, u32[]{:S(2)}) copy-start(f32[8,16,16]{0,2,1:T(8,128)} %copy.177) | copy-start | bytes 24580
  123.3 86.5 %copy-start.10 = (f32[4,16,16]{2,1,0:T(8,128)S(1)}, f32[4,16,16]{2,1,0:T(8,128)}, u32[]{:S(2)}) copy-start(f32[4,16,16]{2,1,0:T(8,128)} %copy-done.9) | copy-start | bytes 12292
  123.3 86.5 %copy-start.11 = (f32[4,16,16]{2,1,0:T(8,128)S(1)}, f32[4,16,16]{2,1,0:T(8,128)}, u32[]{:S(2)}) copy-start(f32[4,16,16]{2,1,0:T(8,128)} %copy.173) | copy-start | bytes 12292
  124.2 121.7 %collective-permute-start.3 = (f32[4,8,1,16,256]{4,3,2,1,0:T(8,128)}, f32[4,8,1,16,256]{4,3,2,1,0:T(8,128)S(1)}, u32[]{:S(2)}, u32[]{:S(2)}) collective-permute-start(f32[4,8,1,16,256]{4,3,2,1,0:T(8,128)} %get-tuple-element.37), channel_id=1, source_target_pairs={{0,1},{1,2},{2,3},{3,4},{4,5},{5,6},{6,7},{8,9},{9,10},{10,11},{11... | collective-permute-start | bytes 1572872 | tf_op jit(solution)/shard_map/ppermute | solution.py:12
  126.9 119.1 %collective-permute-start.2 = (f32[4,8,1,16,256]{4,3,2,1,0:T(8,128)S(1)}, f32[4,8,1,16,256]{4,3,2,1,0:T(8,128)S(1)}, u32[]{:S(2)}, u32[]{:S(2)}) collective-permute-start(f32[4,8,1,16,256]{4,3,2,1,0:T(8,128)S(1)} %get-tuple-element.36), channel_id=1, source_target_pairs={{1,0},{2,1},{3,2},{4,3},{5,4},{6,5},{7,6},{9,8},{10,9},{11,10},{12... | collective-permute-start | bytes 1572872 | tf_op jit(solution)/shard_map/ppermute | solution.py:15
  246.6 0.6 copy-start.15
where the time goes:
time: 250 us; the launch traced here: 249 us
  blocking collectives  116 us (46%)
  local copies, waits for them, and re-layouts  60.2 us (24%)
  waiting for transfers between devices  31.8 us (13%)
  other arithmetic  22 us (9%)
  starting transfers between devices  18 us (7%)
    psum x1, blocking collectives, on_device(): right_total = lax.psum(right_one, ('pair', 'row'))  81.4 us
    psum x1, blocking collectives, on_device(): left_total = lax.psum(left_one, 'row')  34.6 us
    slice x2, local copies, waits for them, and re-layouts, pool_field(): merged = merged[..., 0::2] + merged[..., 1::2]  22.5 us
    ppermute x2, waiting for transfers between devices, padded_2(): lax.ppermute(lax.slice_in_dim(block, 0, width, axis=dim), axis, backward)  12.7 us
    ppermute x2, waiting for transfers between devices, padded_2(): lax.ppermute(lax.slice_in_dim(block, block.shape[dim] - width, None, axis...  9.17 us
    broadcast_in_dim x2, local copies, waits for them, and re-layouts, spread_field(): merged = jnp.broadcast_to(merged, inner + (half_side, 2, half_side, 2))  7.05 us
    add x1, other arithmetic, pool_field(): merged = merged[..., :length] + merged[..., length:]  6.58 us
    ppermute x2, starting transfers between devices, padded_2(): lax.ppermute(lax.slice_in_dim(block, block.shape[dim] - width, None, axis...  6.51 us
  transfers between devices with their start and end apart: 6, of which 4 were waited for; matrix products, arithmetic and copies ran while one was open for 2% of the time, Pallas kernels for 0%

commit v1 on v0

--- a/solution.py
+++ b/solution.py
@@ -2,6 +2,11 @@
 import jax.numpy as jnp
 from jax import lax
 from jax.sharding import PartitionSpec as P
+
+
+def space_time(local_array, peer_axis):
+    moved = lax.all_gather(local_array, axis_name=peer_axis).sum(axis=0)
+    return moved
 
 
 def padded_2(block, sides, width):
@@ -167,7 +172,7 @@
         conv_map(right_two.reshape(count, half_side, half_side))
     ) / 2.0 + right_local.reshape(count, length, length)
     left_total = lax.psum(left_one, "row")
-    right_total = lax.psum(right_one, ("pair", "row"))
+    right_total = space_time(right_one, peer_axis=("pair", "row"))
     return (gram_gradient, conv_map(left_total), conv_map(right_total))
 
 

time: 250 us -> 882 us (3.53)
  waiting for transfers between devices: 31.8 us -> 708 us
  blocking collectives: 116 us -> 44.5 us
  between operations: 1.29 us -> 14.7 us
  other arithmetic: 22 us -> 32.3 us
    all_gather x0 -> x1, waiting for transfers between devices: none -> 676 us  [space_time(): moved = lax.all_gather(local_array, axis_name=peer_axis).sum(axis=0)]
    psum x1 -> x0, blocking collectives: 81.4 us -> none  [on_device(): right_total = lax.psum(right_one, ('pair', 'row'))]
    psum x1, blocking collectives: 34.6 us -> 44.5 us  [on_device(): left_total = lax.psum(left_one, 'row')]
  transfers between devices with their start and end apart: 6 -> 7, of which waited for: 4 -> 5; matrix products, arithmetic and copies ran while one was open for 2% -> 1% of each run, Pallas kernels for 0% -> 0%
where the time goes in v1:
time: 882 us; the launch traced here: 875 us
  waiting for transfers between devices  708 us (80%)
  local copies, waits for them, and re-layouts  57.3 us (6%)
  blocking collectives  44.5 us (5%)
  other arithmetic  32.3 us (4%)
  starting transfers between devices  18 us (2%)
  between operations  14.7 us (2%)
    all_gather x1, waiting for transfers between devices, space_time(): moved = lax.all_gather(local_array, axis_name=peer_axis).sum(axis=0)  676 us
    psum x1, blocking collectives, on_device(): left_total = lax.psum(left_one, 'row')  44.5 us
    slice x2, local copies, waits for them, and re-layouts, pool_field(): merged = merged[..., 0::2] + merged[..., 1::2]  22.5 us
  transfers between devices with their start and end apart: 7, of which 5 were waited for; matrix products, arithmetic and copies ran while one was open for 1% of the time, Pallas kernels for 0%

profile of v1, /device:TPU:2, one launch (start us, length us, event | category | flops | bytes accessed | tf_op | source)
XLA Modules:
  0.0 874.7 jit_solution(13160356678004263511)
XLA Ops:
  7.2 1.4 fusion.60
  8.6 3.9 collective-permute-start.1
  12.5 1.3 collective-permute-start
  16.0 7.6 collective-permute-done.1
  23.6 12.8 %collective-permute-done = f32[4,8,1,16,256]{4,3,2,1,0:T(8,128)S(1)} collective-permute-done((f32[4,8,1,16,256]{4,3,2,1,0:T(8,128)S(1)}, f32[4,8,1,16,256]{4,3,2,1,0:T(8,128)S(1)}, u32[]{:S(2)}, u32[]{:S(2)}) %collective-permute-start) | collective-permute-done | bytes 524320 | tf_op jit(solution)/shard_map/ppermute | solution.py:20
  38.1 0.8 copy-done.2
  39.0 4.2 multiply_multiply_fusion.1
  43.2 3.7 reshape.132
  47.0 6.6 slice_add_fusion
  53.6 3.2 reshape.133
  56.8 11.2 %slice.242 = f32[4,8,2,16,64]{4,3,2,1,0:T(8,128)S(1)} slice(f32[4,8,2,16,128]{4,3,2,1,0:T(8,128)S(1)} %reshape.133), slice={[0:4:1], [0:8:1], [0:2:1], [0:16:1], [0:128:2]} | slice | bytes 524288 | tf_op jit(solution)/shard_map/slice | solution.py:81
  68.0 11.3 %slice.243 = f32[4,8,2,16,64]{4,3,2,1,0:T(8,128)S(1)} slice(f32[4,8,2,16,128]{4,3,2,1,0:T(8,128)S(1)} %reshape.133), slice={[0:4:1], [0:8:1], [0:2:1], [0:16:1], [1:128:2]} | slice | bytes 524288 | tf_op jit(solution)/shard_map/slice | solution.py:81
  80.6 5.5 all-to-all-start
  86.4 6.1 all-to-all-done
  93.0 0.8 reduce.4
  94.1 0.9 fusion.55
  96.4 3.4 all-to-all-start.1
  101.1 4.9 all-to-all-done.1
  106.0 0.8 reduce.5
  108.3 2.2 copy.154
  110.5 3.5 broadcast_in_dim.45
  114.0 3.5 copy.155
  118.2 2.2 copy.146
  120.4 3.5 broadcast_in_dim.19
  123.9 2.8 copy.147
  126.8 2.7 fusion.26
  130.9 2.7 collective-permute-start.3
  133.6 1.3 collective-permute-start.2
  134.9 44.5 %psum.7 = f32[4,16,16]{2,1,0:T(8,128)S(1)} all-reduce(f32[4,16,16]{2,1,0:T(8,128)S(1)} %add_dynamic-update-slice_fusion), channel_id=1, replica_groups=mesh['pair'=32,'row'=8] {'row'}, use_global_device_ids=true, to_apply=%region_6.7 | all-reduce | flops 1024 | bytes 8192 | tf_op jit(solution)/shard_map/psum | solution.py:174
  181.4 2.1 fusion.9
  183.5 676.4 %all-gather.3.cloned.1.call-done = f32[2048,16,16]{2,1,0:T(8,128)} async-done(((f32[8,16,16]{2,1,0:T(8,128)}), f32[2048,16,16]{2,1,0:T(8,128)}) %all-gather.3.cloned.1.call-update) | async-done | bytes 2097168 | tf_op jit(solution)/shard_map/all_gather | solution.py:8
  860.0 7.1 reduce_sum.94
  (113 shorter events, 15.0 us)
Async XLA Ops:
  7.2 30.0 %copy-start = (f32[4,8,2,16,256]{4,3,2,1,0:T(8,128)S(1)}, f32[4,8,2,16,256]{4,3,2,1,0:T(8,128)}, u32[]{:S(2)}) copy-start(f32[4,8,2,16,256]{4,3,2,1,0:T(8,128)} %param.4) | copy-start | bytes 3145732
  7.2 6.6 copy-start.12
  7.2 6.8 copy-start.13
  8.6 15.0 %collective-permute-start.1 = (f32[4,8,1,16,256]{4,3,2,1,0:T(8,128)S(1)}, f32[4,8,1,16,256]{4,3,2,1,0:T(8,128)S(1)}, u32[]{:S(2)}, u32[]{:S(2)}) collective-permute-start(f32[4,8,1,16,256]{4,3,2,1,0:T(8,128)S(1)} %get-tuple-element.26), channel_id=1, source_target_pairs={{0,1},{1,2},{2,3},{3,4},{4,5},{5,6},{6,7},{8,9},{9,10},{10,11},{11... | collective-permute-start | bytes 1572872 | tf_op jit(solution)/shard_map/ppermute | solution.py:17
  12.5 23.9 %collective-permute-start = (f32[4,8,1,16,256]{4,3,2,1,0:T(8,128)S(1)}, f32[4,8,1,16,256]{4,3,2,1,0:T(8,128)S(1)}, u32[]{:S(2)}, u32[]{:S(2)}) collective-permute-start(f32[4,8,1,16,256]{4,3,2,1,0:T(8,128)S(1)} %get-tuple-element.25), channel_id=1, source_target_pairs={{1,0},{2,1},{3,2},{4,3},{5,4},{6,5},{7,6},{9,8},{10,9},{11,10},{12... | collective-permute-start | bytes 1572872 | tf_op jit(solution)/shard_map/ppermute | solution.py:20
  15.4 22.7 %copy-start.14 = (f32[256]{0:T(256)}, f32[256]{0:T(256)S(1)}, u32[]{:S(2)}) copy-start(f32[256]{0:T(256)S(1)} %get-tuple-element.42) | copy-start | bytes 3076
  23.6 12.8 %copy-start.1 = (f32[4,8,1,16,256]{4,3,2,1,0:T(8,128)}, f32[4,8,1,16,256]{4,3,2,1,0:T(8,128)S(1)}, u32[]{:S(2)}) copy-start(f32[4,8,1,16,256]{4,3,2,1,0:T(8,128)S(1)} %collective-permute-done.1) | copy-start | bytes 1572868
  36.4 0.8 copy-start.3
  37.8 1.0 copy-start.2
  37.8 1.2 copy-start.4
  56.8 29.3 %copy-start.9 = (f32[8,64]{0,1:T(8,128)S(1)}, f32[8,64]{0,1:T(8,128)}, u32[]{:S(2)}) copy-start(f32[8,64]{0,1:T(8,128)} %fusion.49) | copy-start | bytes 6148
  56.8 29.4 %copy-start.10 = (f32[4,8,8]{0,2,1:T(8,128)S(1)}, f32[4,8,8]{0,2,1:T(8,128)}, u32[]{:S(2)}) copy-start(f32[4,8,8]{0,2,1:T(8,128)} %fusion.45) | copy-start | bytes 3076
  79.3 14.7 %copy-start.7 = (f32[4,1,8,8,64]{4,3,2,1,0:T(8,128)S(1)}, f32[4,1,8,8,64]{4,3,2,1,0:T(8,128)}, u32[]{:S(2)}) copy-start(f32[4,1,8,8,64]{4,3,2,1,0:T(8,128)} %param.7) | copy-start | bytes 196612
  80.6 11.9 %all-to-all-start = ((f32[8,1,2048]{2,1,0:T(1,128)}), f32[8,1,2048]{2,1,0:T(1,128)S(1)}, u32[]{:S(2)}, u32[]{:S(2)}) async-start(f32[8,1,2048]{2,1,0:T(1,128)} %reshape.139), calls=%async_computation | async-start | bytes 131072 | tf_op jit(solution)/shard_map/all_to_all | solution.py:144
  96.4 9.6 %all-to-all-start.1 = ((f32[8,1,2048]{2,1,0:T(1,128)}), f32[8,1,2048]{2,1,0:T(1,128)S(1)}, u32[]{:S(2)}, u32[]{:S(2)}) async-start(f32[8,1,2048]{2,1,0:T(1,128)} %reshape.141), calls=%async_computation.1 | async-start | bytes 131072 | tf_op jit(solution)/shard_map/all_to_all | solution.py:158
  99.8 760.2 %all-gather.3.cloned.1.call-start = ((), (), s32[]{:S(2)}) async-start(), calls=%async_computation.2 | async-start | bytes 16842752 | tf_op jit(solution)/shard_map/all_gather | solution.py:8
  114.0 3.6 copy-start.6
  123.9 2.9 copy-start.5
  126.8 2.8 copy-start.8
  126.8 3.5 copy-start.11
  130.9 49.3 %collective-permute-start.3 = (f32[4,8,1,16,256]{4,3,2,1,0:T(8,128)S(1)}, f32[4,8,1,16,256]{4,3,2,1,0:T(8,128)S(1)}, u32[]{:S(2)}, u32[]{:S(2)}) collective-permute-start(f32[4,8,1,16,256]{4,3,2,1,0:T(8,128)S(1)} %get-tuple-element.22), channel_id=1, source_target_pairs={{0,1},{1,2},{2,3},{3,4},{4,5},{5,6},{6,7},{8,9},{9,10},{10,11},{11... | collective-permute-start | bytes 1572872 | tf_op jit(solution)/shard_map/ppermute | solution.py:17
  133.6 46.6 %collective-permute-start.2 = (f32[4,8,1,16,256]{4,3,2,1,0:T(8,128)S(1)}, f32[4,8,1,16,256]{4,3,2,1,0:T(8,128)S(1)}, u32[]{:S(2)}, u32[]{:S(2)}) collective-permute-start(f32[4,8,1,16,256]{4,3,2,1,0:T(8,128)S(1)} %get-tuple-element.21), channel_id=1, source_target_pairs={{1,0},{2,1},{3,2},{4,3},{5,4},{6,5},{7,6},{9,8},{10,9},{11,10},{12... | collective-permute-start | bytes 1572872 | tf_op jit(solution)/shard_map/ppermute | solution.py:20
  180.7 0.7 copy-start.15
Sparse Core Ops, SparseCore 0:
  130.4 729.5 all-gather.2
